TPU v7x, 32 devices: a whole 2x2x4 slice. The times are simulated.
32 devices in a mesh: fsdp: 2 (over x), ctx: 4 (over y, core), tp: 4 (over z).
Axes of the slice: x: 2, y: 2, z: 4, core: 2. Of those that a mesh axis runs over, the one named last changes fastest.
Arguments:
- block_in: bfloat16 [8, 1024, 2048], P('fsdp', 'ctx', 'tp'), may hold values from -6 to 6
- seg_ids: int32 [8, 1024], P('fsdp'), may hold values from 0 to 7, never falling along the last dimension, each value on 1 to 512 neighbouring positions
- out_cot: bfloat16 [8, 1024, 2048], P('fsdp', 'ctx'), may hold values from -6 to 6
- norm_gain: bfloat16 [2048], P('tp'), may hold values from 0.099609375 to 1.8984375
- mid_gain: bfloat16 [2048], P('tp'), may hold values from 0.099609375 to 1.8984375
- gelu_proj: bfloat16 [2048, 2816], P(('fsdp', 'ctx'), 'tp'), may hold values from -0.125 to 0.125
- scan_proj: bfloat16 [2048, 2816], P(('fsdp', 'ctx'), 'tp'), may hold values from -0.125 to 0.125
- out_proj: bfloat16 [2816, 2048], P('tp', ('fsdp', 'ctx')), may hold values from -0.4375 to 0.4375
- gate_proj: bfloat16 [2048, 6144], P(('fsdp', 'ctx'), 'tp'), may hold values from -0.125 to 0.125
- up_proj: bfloat16 [2048, 6144], P(('fsdp', 'ctx'), 'tp'), may hold values from -0.125 to 0.125
- down_proj: bfloat16 [6144, 2048], P('tp', ('fsdp', 'ctx')), may hold values from -0.109375 to 0.109375
- conv_kernel: float32 [4, 2816], P(None, 'tp'), may hold values from -3 to 3
- conv_bias: float32 [2816], P('tp'), may hold values from -3 to 3
- rate_gate: bfloat16 [16, 176, 176], P('tp'), may hold values from -0.4375 to 0.4375
- input_gate: bfloat16 [16, 176, 176], P('tp'), may hold values from -0.4375 to 0.4375
- rate_bias: float32 [2816], P('tp'), may hold values from -4 to 4
- input_bias: float32 [2816], P('tp'), may hold values from -4 to 4
- decay_param: float32 [2816], P('tp'), may hold values from -16 to -4
Outputs:
- block_out: bfloat16 [8, 1024, 2048], P('fsdp', 'ctx', 'tp')
- grad_in: float32 [8, 1024, 2048], P('fsdp', 'ctx', 'tp')
- grad_norm_gain: float32 [2048], P('tp')
- grad_mid_gain: float32 [2048], P('tp')
- grad_gelu_proj: float32 [2048, 2816], P(('fsdp', 'ctx'), 'tp')
- grad_scan_proj: float32 [2048, 2816], P(('fsdp', 'ctx'), 'tp')
- grad_out_proj: float32 [2816, 2048], P('tp', ('fsdp', 'ctx'))
- grad_gate_proj: float32 [2048, 6144], P(('fsdp', 'ctx'), 'tp')
- grad_up_proj: float32 [2048, 6144], P(('fsdp', 'ctx'), 'tp')
- grad_down_proj: float32 [6144, 2048], P('tp', ('fsdp', 'ctx'))
- grad_conv_kernel: float32 [4, 2816], P(None, 'tp')
- grad_conv_bias: float32 [2816], P('tp')
- grad_rate_gate: float32 [16, 176, 176], P('tp')
- grad_input_gate: float32 [16, 176, 176], P('tp')
- grad_rate_bias: float32 [2816], P('tp')
- grad_input_bias: float32 [2816], P('tp')
- grad_decay_param: float32 [2816], P('tp')
Inputs may be any that keep to these rules, and one draw needn't show every extreme that they name: `seg_ids`: in every row the document numbers never fall; each of the 8 documents covers 1 to 512 positions, and one covers exactly 512.
All inputs are finite; a program needn't handle non-finite values.
Results may differ from a plain program's by a relative error of at most 0.0095.
Values may be sent and summed in bfloat16 or wider, within the bound.
A program may use at most 320 MiB of HBM per device.

v0:
```python
import jax
import jax.numpy as jnp
from jax import lax
from jax.sharding import PartitionSpec as P

CONV = 4
eps_norm = 1e-06


def from_behind(value, axis, steps):
    count = lax.axis_size(axis)
    leading, last = (max(0, -steps), min(count, count - steps))
    return lax.ppermute(value, axis, [(source, source + steps) for source in range(leading, last)])


def entering(value, axis, join, neutral, backward):
    count, mine = (lax.axis_size(axis), lax.axis_index(axis))
    pieces = jax.tree.map(lambda part: lax.all_gather(part, axis), value)
    if backward:
        pieces = jax.tree.map(lambda part: part[::-1], pieces)
        mine = count - 1 - mine
    total = jax.tree.map(
        lambda part, zero: jnp.full_like(part, 0) + jnp.asarray(zero, part.dtype), value, neutral
    )

    def step(position, total):
        longer = join(total, jax.tree.map(lambda part: part[position], pieces))
        return jax.tree.map(lambda new, old: jnp.where(position < mine, new, old), longer, total)

    return lax.fori_loop(0, count - 1, step, total)


def rms_scale(values, gain_vec):
    return (
        values * lax.rsqrt(jnp.mean(values * values, axis=-1, keepdims=True) + eps_norm) * gain_vec
    )


def gelu_tanh(values):
    return jax.nn.gelu(values, approximate=True)


def gate_values(pre_rate, pre_input, decay_param):
    rate_vals = jax.nn.sigmoid(pre_rate)
    input_vals = jax.nn.sigmoid(pre_input)
    log_a = -8.0 * jax.nn.softplus(decay_param) * rate_vals
    return (jnp.exp(log_a), jnp.sqrt(-jnp.expm1(2.0 * log_a)) * input_vals)


def combine(first_part, second_part):
    return (first_part[0] * second_part[0], second_part[0] * first_part[1] + second_part[1])


def matmul(left, right):
    return jnp.dot(left, right, preferred_element_type=jnp.float32)


def matmul_rt(left, right):
    return lax.dot_general(
        left, right, (((1,), (1,)), ((), ())), preferred_element_type=jnp.float32
    )


def matmul_lt(left, right):
    return lax.dot_general(
        left, right, (((0,), (0,)), ((), ())), preferred_element_type=jnp.float32
    )


def shards(
    block_in,
    seg_ids,
    out_cot,
    norm_gain,
    mid_gain,
    gelu_proj,
    scan_proj,
    out_proj,
    gate_proj,
    up_proj,
    down_proj,
    conv_kernel,
    conv_bias,
    rate_gate,
    input_gate,
    rate_bias,
    input_bias,
    decay_param,
):
    seq_count, tok_count, part_width = block_in.shape
    row_count = seq_count * tok_count
    full_in, gain_one, gain_two = (
        lax.all_gather(block_in, "tp", axis=2, tiled=True),
        lax.all_gather(norm_gain, "tp", axis=0, tiled=True),
        lax.all_gather(mid_gain, "tp", axis=0, tiled=True),
    )
    w_gelu, w_scan, w_out, w_gate, w_up, w_down = (
        lax.all_gather(gelu_proj, ("fsdp", "ctx"), axis=0, tiled=True),
        lax.all_gather(scan_proj, ("fsdp", "ctx"), axis=0, tiled=True),
        lax.all_gather(out_proj, ("fsdp", "ctx"), axis=1, tiled=True),
        lax.all_gather(gate_proj, ("fsdp", "ctx"), axis=0, tiled=True),
        lax.all_gather(up_proj, ("fsdp", "ctx"), axis=0, tiled=True),
        lax.all_gather(down_proj, ("fsdp", "ctx"), axis=1, tiled=True),
    )
    full_width = full_in.shape[2]
    rec_width = w_gelu.shape[1]
    head_count = rate_gate.shape[0]
    head_size = rate_gate.shape[1]
    x_rows = full_in.reshape(row_count, full_width).astype(jnp.float32)
    normed_f, norm_one_back = jax.vjp(rms_scale, x_rows, gain_one.astype(jnp.float32))
    normed = normed_f.astype(jnp.bfloat16)
    y_pre = matmul(normed, w_gelu)
    y_act, y_back = jax.vjp(gelu_tanh, y_pre)
    x_branch = matmul(normed, w_scan).astype(jnp.bfloat16).reshape(seq_count, tok_count, rec_width)
    margin_len = CONV - 1
    start_tok = lax.axis_index("ctx") * tok_count
    padded_ids = jnp.concatenate(
        [
            jnp.full((seq_count, margin_len), -1, jnp.int32),
            seg_ids,
            jnp.full((seq_count, margin_len), -2, jnp.int32),
        ],
        axis=1,
    )
    window_ids = lax.dynamic_slice_in_dim(padded_ids, start_tok, tok_count + 2 * margin_len, 1)
    own_ids = window_ids[:, margin_len : margin_len + tok_count]
    back_masks = [
        (window_ids[:, margin_len - offset : margin_len - offset + tok_count] == own_ids).astype(
            jnp.float32
        )[..., None]
        for offset in range(CONV)
    ]
    ahead_masks = [
        (window_ids[:, margin_len + offset : margin_len + offset + tok_count] == own_ids).astype(
            jnp.float32
        )[..., None]
        for offset in range(CONV)
    ]
    prev_edge = from_behind(x_branch[:, tok_count - margin_len :, :], "ctx", 1)
    ext_x = jnp.concatenate([prev_edge, x_branch], axis=1)
    conv_sum = conv_bias + jnp.zeros((seq_count, tok_count, rec_width), jnp.float32)
    for offset in range(CONV):
        conv_sum = (
            conv_sum
            + conv_kernel[offset]
            * ext_x[:, margin_len - offset : margin_len - offset + tok_count].astype(jnp.float32)
            * back_masks[offset]
        )
    conv_out = conv_sum.astype(jnp.bfloat16)
    conv_vals = conv_out.astype(jnp.float32)
    heads_in = conv_out.reshape(row_count, head_count, head_size)
    pre_rate = (
        jnp.einsum("rhi,hij->rhj", heads_in, rate_gate, preferred_element_type=jnp.float32).reshape(
            row_count, rec_width
        )
        + rate_bias
    )
    pre_input = (
        jnp.einsum(
            "rhi,hij->rhj", heads_in, input_gate, preferred_element_type=jnp.float32
        ).reshape(row_count, rec_width)
        + input_bias
    )
    (decays, in_scale), gate_back = jax.vjp(gate_values, pre_rate, pre_input, decay_param)
    in_scale3 = in_scale.reshape(seq_count, tok_count, rec_width)
    coeffs = decays.reshape(seq_count, tok_count, rec_width) * back_masks[1]
    inputs = in_scale3 * conv_vals
    cum_coef, local_state = lax.associative_scan(combine, (coeffs, inputs), axis=1)
    ones_row = jnp.ones((seq_count, rec_width), jnp.float32)
    zeros_row = jnp.zeros((seq_count, rec_width), jnp.float32)
    _, state_in = entering(
        (cum_coef[:, -1], local_state[:, -1]), "ctx", combine, (ones_row, zeros_row), False
    )
    states = local_state + cum_coef * state_in[:, None, :]
    state_rows = states.reshape(row_count, rec_width)
    mixed_in = (state_rows * y_act).astype(jnp.bfloat16)
    rec_part = matmul(mixed_in, w_out)
    col_start = lax.axis_index("tp") * part_width
    rec_total = lax.psum(rec_part, "tp")
    mid_rows = x_rows + rec_total
    normed_mid_f, norm_two_back = jax.vjp(rms_scale, mid_rows, gain_two.astype(jnp.float32))
    normed_mid = normed_mid_f.astype(jnp.bfloat16)
    gate_pre = matmul(normed_mid, w_gate)
    up_pre = matmul(normed_mid, w_up)
    gate_act, gate_act_back = jax.vjp(gelu_tanh, gate_pre)
    hidden = (gate_act * up_pre).astype(jnp.bfloat16)
    mlp_slice = lax.psum_scatter(matmul(hidden, w_down), "tp", scatter_dimension=1, tiled=True)
    mid_own = lax.dynamic_slice_in_dim(mid_rows, col_start, part_width, 1)
    block_out = (mid_own + mlp_slice).astype(jnp.bfloat16).reshape(seq_count, tok_count, part_width)
    cot_rows = out_cot.reshape(row_count, full_width)
    hid_grad = matmul_rt(cot_rows, w_down)
    grad_down = matmul_lt(hidden, cot_rows)
    gate_grad = gate_act_back(hid_grad * up_pre)[0].astype(jnp.bfloat16)
    up_grad = (hid_grad * gate_act).astype(jnp.bfloat16)
    grad_gate = matmul_lt(normed_mid, gate_grad)
    grad_up = matmul_lt(normed_mid, up_grad)
    mid_part = matmul_rt(gate_grad, w_gate) + matmul_rt(up_grad, w_up)
    mid_norm_grad = lax.psum(mid_part, "tp")
    mid_from_norm, gain_two_grad = norm_two_back(mid_norm_grad)
    mid_grad = cot_rows.astype(jnp.float32) + mid_from_norm
    rec_grad = mid_grad.astype(jnp.bfloat16)
    mixed_grad = matmul_rt(rec_grad, w_out)
    grad_out = matmul_lt(mixed_in, rec_grad)
    state_direct = (mixed_grad * y_act).reshape(seq_count, tok_count, rec_width)
    y_grad = y_back(mixed_grad * state_rows)[0].astype(jnp.bfloat16)
    grad_gelu = matmul_lt(normed, y_grad)
    in_part = matmul_rt(y_grad, w_gelu)
    next_coef = jnp.concatenate(
        [coeffs[:, 1:], jnp.ones((seq_count, 1, rec_width), jnp.float32)], axis=1
    )
    tail_coef, local_grad = lax.associative_scan(
        combine, (next_coef, state_direct), reverse=True, axis=1
    )
    head_coef = coeffs[:, 0]
    _, grad_in_state = entering(
        (head_coef * tail_coef[:, 0], head_coef * local_grad[:, 0]),
        "ctx",
        combine,
        (ones_row, zeros_row),
        True,
    )
    state_grad = local_grad + tail_coef * grad_in_state[:, None, :]
    prev_states = jnp.concatenate([state_in[:, None, :], states[:, :-1]], axis=1)
    decay_grad = (state_grad * prev_states * back_masks[1]).reshape(row_count, rec_width)
    scale_grad = (state_grad * conv_vals).reshape(row_count, rec_width)
    conv_direct = (state_grad * in_scale3).reshape(row_count, rec_width)
    rate_raw, input_raw, grad_decay = gate_back((decay_grad, scale_grad))
    rate_grad = rate_raw.astype(jnp.bfloat16)
    input_grad = input_raw.astype(jnp.bfloat16)
    rate_heads = rate_grad.reshape(row_count, head_count, head_size)
    input_heads = input_grad.reshape(row_count, head_count, head_size)
    grad_rate_gate = jnp.einsum(
        "rhi,rhj->hij", heads_in, rate_heads, preferred_element_type=jnp.float32
    )
    grad_input_gate = jnp.einsum(
        "rhi,rhj->hij", heads_in, input_heads, preferred_element_type=jnp.float32
    )
    grad_rate_bias = jnp.sum(rate_grad.astype(jnp.float32), axis=0)
    grad_input_bias = jnp.sum(input_grad.astype(jnp.float32), axis=0)
    gate_back_in = jnp.einsum(
        "rhj,hij->rhi", rate_heads, rate_gate, preferred_element_type=jnp.float32
    ) + jnp.einsum("rhj,hij->rhi", input_heads, input_gate, preferred_element_type=jnp.float32)
    conv_grad = (
        (conv_direct + gate_back_in.reshape(row_count, rec_width))
        .astype(jnp.bfloat16)
        .reshape(seq_count, tok_count, rec_width)
    )
    next_edge = from_behind(conv_grad[:, :margin_len, :], "ctx", -1)
    ext_grad = jnp.concatenate([conv_grad, next_edge], axis=1)
    conv_grad_f = conv_grad.astype(jnp.float32)
    branch_grad = jnp.zeros((seq_count, tok_count, rec_width), jnp.float32)
    kernel_rows = []
    for offset in range(CONV):
        branch_grad = (
            branch_grad
            + conv_kernel[offset]
            * ext_grad[:, offset : offset + tok_count].astype(jnp.float32)
            * ahead_masks[offset]
        )
        kernel_rows.append(
            jnp.sum(
                conv_grad_f
                * ext_x[:, margin_len - offset : margin_len - offset + tok_count].astype(
                    jnp.float32
                )
                * back_masks[offset],
                axis=(0, 1),
            )
        )
    grad_kernel = jnp.stack(kernel_rows)
    grad_conv = jnp.sum(conv_grad_f, axis=(0, 1))
    branch_low = branch_grad.astype(jnp.bfloat16).reshape(row_count, rec_width)
    grad_scan = matmul_lt(normed, branch_low)
    in_part = in_part + matmul_rt(branch_low, w_scan)
    in_from_norm, gain_one_part = norm_one_back(in_part)
    in_slice, gain_one_slice = (
        lax.psum_scatter(in_from_norm, "tp", scatter_dimension=1, tiled=True),
        lax.psum_scatter(gain_one_part, "tp", scatter_dimension=0, tiled=True),
    )
    grad_in = (lax.dynamic_slice_in_dim(mid_grad, col_start, part_width, 1) + in_slice).reshape(
        seq_count, tok_count, part_width
    )
    gain_two_slice = lax.dynamic_slice_in_dim(gain_two_grad, col_start, part_width, 0)
    grad_gelu_s, grad_scan_s, grad_out_s, grad_gate_s, grad_up_s, grad_down_s = (
        lax.psum_scatter(grad_gelu, ("fsdp", "ctx"), scatter_dimension=0, tiled=True),
        lax.psum_scatter(grad_scan, ("fsdp", "ctx"), scatter_dimension=0, tiled=True),
        lax.psum_scatter(grad_out, ("fsdp", "ctx"), scatter_dimension=1, tiled=True),
        lax.psum_scatter(grad_gate, ("fsdp", "ctx"), scatter_dimension=0, tiled=True),
        lax.psum_scatter(grad_up, ("fsdp", "ctx"), scatter_dimension=0, tiled=True),
        lax.psum_scatter(grad_down, ("fsdp", "ctx"), scatter_dimension=1, tiled=True),
    )
    (
        gain_one_total,
        gain_two_total,
        kernel_total,
        conv_total,
        rate_gate_total,
        input_gate_total,
        rate_bias_total,
        input_bias_total,
        decay_total,
    ) = lax.psum(
        (
            gain_one_slice,
            gain_two_slice,
            grad_kernel,
            grad_conv,
            grad_rate_gate,
            grad_input_gate,
            grad_rate_bias,
            grad_input_bias,
            grad_decay,
        ),
        ("fsdp", "ctx"),
    )
    return (
        block_out,
        grad_in,
        gain_one_total,
        gain_two_total,
        grad_gelu_s,
        grad_scan_s,
        grad_out_s,
        grad_gate_s,
        grad_up_s,
        grad_down_s,
        kernel_total,
        conv_total,
        rate_gate_total,
        input_gate_total,
        rate_bias_total,
        input_bias_total,
        decay_total,
    )


def solution(mesh):
    in_specs = (
        P("fsdp", "ctx", "tp"),
        P("fsdp", None),
        P("fsdp", "ctx", None),
        P("tp"),
        P("tp"),
        P(("fsdp", "ctx"), "tp"),
        P(("fsdp", "ctx"), "tp"),
        P("tp", ("fsdp", "ctx")),
        P(("fsdp", "ctx"), "tp"),
        P(("fsdp", "ctx"), "tp"),
        P("tp", ("fsdp", "ctx")),
        P(None, "tp"),
        P("tp"),
        P("tp", None, None),
        P("tp", None, None),
        P("tp"),
        P("tp"),
        P("tp"),
    )
    out_specs = (
        P("fsdp", "ctx", "tp"),
        P("fsdp", "ctx", "tp"),
        P("tp"),
        P("tp"),
        P(("fsdp", "ctx"), "tp"),
        P(("fsdp", "ctx"), "tp"),
        P("tp", ("fsdp", "ctx")),
        P(("fsdp", "ctx"), "tp"),
        P(("fsdp", "ctx"), "tp"),
        P("tp", ("fsdp", "ctx")),
        P(None, "tp"),
        P("tp"),
        P("tp", None, None),
        P("tp", None, None),
        P("tp"),
        P("tp"),
        P("tp"),
    )
    return jax.shard_map(shards, mesh=mesh, in_specs=in_specs, out_specs=out_specs, check_vma=False)
```

profile of v0, /device:TPU:0, one launch (start us, length us, event | category | flops | bytes accessed | tf_op | source)
XLA Modules:
  0.0 2524.0 jit_solution(14394685174451569282)
XLA Ops:
  10.7 13.5 all-gather.4
  26.8 66.3 %all-gather.14.cloned.1.call-done = bf16[4,256,2048]{2,1,0:T(8,128)(2,1)} async-done(((bf16[4,256,512]{2,1,0:T(8,128)(2,1)}), bf16[4,256,2048]{2,1,0:T(8,128)(2,1)}) %all-gather.14.cloned.1.call-update) | async-done | bytes 4194320 | tf_op jit(solution)/shard_map/all_gather | solution.py:93
  100.0 25.2 all-gather.16.cloned.1.call-done
  125.2 6.3 convolution_convert_fusion
  172.3 7.0 convert_multiply_fusion.8
  179.3 10.2 slice.580
  189.5 9.6 slice.581
  374.8 9.6 slice.635
  474.3 5.8 pad.212
  489.6 5.7 pad.229
  498.1 5.9 pad.228
  505.0 5.8 all-gather
  516.0 7.5 multiply_add_fusion.2
  527.0 9.7 multiply_convert_fusion.3
  536.7 9.1 fusion.116
  547.9 12.2 all-gather.5
  560.1 277.4 %all-reduce.73.cloned.1.call-done = f32[1024,2048]{1,0:T(8,128)} async-done(((f32[1024,2048]{1,0:T(8,128)}), f32[1024,2048]{1,0:T(8,128)}) %all-reduce.73.cloned.1.call-update) | async-done | bytes 8388624 | tf_op jit(solution)/shard_map/psum | solution.py:179
  837.5 5.9 multiply_reduce_fusion.2
  849.7 34.1 %all-gather.22.cloned.1.call-done = bf16[2048,1536]{1,0:T(8,128)(2,1)} async-done(((bf16[256,1536]{1,0:T(8,128)(2,1)}), bf16[2048,1536]{1,0:T(8,128)(2,1)}) %all-gather.22.cloned.1.call-update) | async-done | bytes 6291472 | tf_op jit(solution)/shard_map/all_gather | solution.py:101
  883.8 11.8 fusion.117
  895.7 35.6 %all-gather.24.cloned.1.call-done = bf16[2048,1536]{1,0:T(8,128)(2,1)} async-done(((bf16[256,1536]{1,0:T(8,128)(2,1)}), bf16[2048,1536]{1,0:T(8,128)(2,1)}) %all-gather.24.cloned.1.call-update) | async-done | bytes 6291472 | tf_op jit(solution)/shard_map/all_gather | solution.py:102
  931.3 11.9 fusion.118
  943.1 36.7 %all-gather.26.cloned.1.call-done = bf16[1536,2048]{1,0:T(8,128)(2,1)} async-done(((bf16[1536,256]{1,0:T(8,128)(2,1)}), bf16[1536,2048]{1,0:T(8,128)(2,1)}) %all-gather.26.cloned.1.call-update) | async-done | bytes 6291472 | tf_op jit(solution)/shard_map/all_gather | solution.py:103
  979.9 18.6 multiply_convert_fusion.1
  998.4 10.0 fusion.120
  1008.5 10.9 convolution_add_fusion.1
  1023.8 9.7 slice.657
  1033.4 9.6 slice.664
  1043.0 9.5 slice.655
  1053.1 12.8 slice.658
  1065.9 12.7 slice.665
  1078.7 12.8 slice.656
  1091.5 11.9 fusion.119
  1103.5 206.9 %all-reduce.75.cloned.1.call-done = f32[1024,2048]{1,0:T(8,128)} async-done(((f32[1024,2048]{1,0:T(8,128)}), f32[1024,2048]{1,0:T(8,128)}) %all-reduce.75.cloned.1.call-update) | async-done | bytes 8388624 | tf_op jit(solution)/shard_map/psum | solution.py:198
  1310.4 7.7 multiply_reduce_fusion
  1325.5 11.8 fusion.72
  1340.8 9.5 slice.659
  1350.4 9.6 slice.661
  1359.9 12.8 slice.660
  1372.7 12.8 slice.662
  1480.8 9.5 slice.717
  1641.5 12.8 slice.718
  1669.5 5.7 pad.260
  1695.7 24.7 rev.15
  1720.5 24.8 rev.14
  1747.6 11.8 multiply_reduce_fusion.3
  1778.6 7.5 fusion.60
  1799.5 10.8 fusion.43
  1831.7 9.1 fusion.62
  1842.2 7.3 fusion.128
  1850.9 8.0 fusion.22
  1859.0 12.5 fusion.122
  1871.8 12.6 fusion.123
  1884.4 12.2 fusion.124
  1899.4 9.0 all-reduce.66
  1908.5 26.4 %all-reduce.67 = (f32[512]{0:T(512)}, f32[512]{0:T(512)}, f32[4,704]{1,0:T(4,128)}, f32[704]{0:T(1024)}, f32[704]{0:T(1024)}, /*index=5*/f32[704]{0:T(1024)}, f32[704]{0:T(1024)}) all-reduce(f32[512]{0:T(512)S(1)} %dynamic-slice.3, f32[512]{0:T(512)S(1)} %dynamic_slice.43, ...), channel_id=1, replica_groups=mesh['fsdp'=2,'ctx'=4,'tp'=4] {'fsdp','ctx'}, use_global_device_ids=true, to_apply=%region_14.15 | all-reduce | flops 6656 | bytes 53248 | tf_op jit(solution)/shard_map/psum | solution.py:302
  1938.5 33.6 %reduce-scatter.11.cloned.1.call-done = f32[1024,512]{1,0:T(8,128)} async-done(((f32[1024,2048]{1,0:T(8,128)}), f32[1024,512]{1,0:T(8,128)}) %reduce-scatter.11.cloned.1.call-update) | async-done | bytes 2097168 | tf_op jit(solution)/shard_map/reduce_scatter | solution.py:277
  1976.2 58.8 %all-reduce.77.cloned.1.call-done = (f32[4,176,176]{2,1,0:T(8,128)}, f32[4,176,176]{2,1,0:T(8,128)}) async-done(((f32[4,176,176]{2,1,0:T(8,128)}, f32[4,176,176]{2,1,0:T(8,128)}), (f32[4,176,176]{2,1,0:T(8,128)}, f32[4,176,176]{2,1,0:T(8,128)})) %all-reduce.77.cloned.1.call-update) | async-done | bytes 991248 | tf_op jit(solution)/shard_map/psum | solution.py:302
  2034.9 62.7 %reduce-scatter.17.cloned.1.call-done = f32[704,256]{1,0:T(8,128)} async-done(((f32[704,2048]{1,0:T(8,128)}), f32[704,256]{1,0:T(8,128)}) %reduce-scatter.17.cloned.1.call-update) | async-done | bytes 720912 | tf_op jit(solution)/shard_map/reduce_scatter | solution.py:287
  2097.6 63.0 %reduce-scatter.13.cloned.1.call-done = f32[256,704]{0,1:T(8,128)} async-done(((f32[2048,704]{0,1:T(8,128)}), f32[256,704]{0,1:T(8,128)}) %reduce-scatter.13.cloned.1.call-update) | async-done | bytes 720912 | tf_op jit(solution)/shard_map/reduce_scatter | solution.py:285
  2160.6 63.3 %reduce-scatter.15.cloned.1.call-done = f32[256,704]{0,1:T(8,128)} async-done(((f32[2048,704]{0,1:T(8,128)}), f32[256,704]{0,1:T(8,128)}) %reduce-scatter.15.cloned.1.call-update) | async-done | bytes 720912 | tf_op jit(solution)/shard_map/reduce_scatter | solution.py:286
  2223.9 96.3 %reduce-scatter.19.cloned.1.call-done = f32[256,1536]{1,0:T(8,128)} async-done(((f32[2048,1536]{1,0:T(8,128)}), f32[256,1536]{1,0:T(8,128)}) %reduce-scatter.19.cloned.1.call-update) | async-done | bytes 1572880 | tf_op jit(solution)/shard_map/reduce_scatter | solution.py:288
  2320.2 96.3 %reduce-scatter.21.cloned.1.call-done = f32[256,1536]{1,0:T(8,128)} async-done(((f32[2048,1536]{1,0:T(8,128)}), f32[256,1536]{1,0:T(8,128)}) %reduce-scatter.21.cloned.1.call-update) | async-done | bytes 1572880 | tf_op jit(solution)/shard_map/reduce_scatter | solution.py:289
  2416.5 96.4 %reduce-scatter.23.cloned.1.call-done = f32[1536,256]{1,0:T(8,128)} async-done(((f32[1536,2048]{1,0:T(8,128)}), f32[1536,256]{1,0:T(8,128)}) %reduce-scatter.23.cloned.1.call-update) | async-done | bytes 1572880 | tf_op jit(solution)/shard_map/reduce_scatter | solution.py:290
  (599 shorter events, 724.4 us)
Async XLA Ops:
  7.2 141.0 %copy-start = (bf16[4,176,176]{2,1,0:T(8,128)(2,1)S(1)}, bf16[4,176,176]{2,1,0:T(8,128)(2,1)}, u32[]{:S(2)}) copy-start(bf16[4,176,176]{2,1,0:T(8,128)(2,1)} %param.35) | copy-start | bytes 743428
  7.2 85.9 %all-gather.14.cloned.1.call-start = ((), (), s32[]{:S(2)}) async-start(), calls=%async_computation.8 | async-start | bytes 5242880 | tf_op jit(solution)/shard_map/all_gather | solution.py:93
  7.9 117.3 %all-gather.16.cloned.1.call-start = ((), (), s32[]{:S(2)}) async-start(), calls=%async_computation.9 | async-start | bytes 3244032 | tf_op jit(solution)/shard_map/all_gather | solution.py:99
  8.7 518.3 %all-gather.18.cloned.1.call-start = ((), (), s32[]{:S(2)}) async-start(), calls=%async_computation.10 | async-start | bytes 3244032 | tf_op jit(solution)/shard_map/all_gather | solution.py:98
  9.4 527.2 %all-gather.20.cloned.1.call-start = ((), (), s32[]{:S(2)}) async-start(), calls=%async_computation.11 | async-start | bytes 3244032 | tf_op jit(solution)/shard_map/all_gather | solution.py:100
  10.0 827.5 %all-reduce.73.cloned.1.call-start = ((), (), s32[]{:S(2)}) async-start(), calls=%async_computation.12 | async-start | bytes 16777216 | tf_op jit(solution)/shard_map/psum | solution.py:179
  24.3 75.8 %copy-start.51 = (f32[4,1,512]{2,1,0:T(1,128)}, f32[4,1,512]{2,1,0:T(1,128)S(1)}, u32[]{:S(2)}) copy-start(f32[4,1,512]{2,1,0:T(1,128)S(1)} %convert_element_type.180) | copy-start | bytes 24580
  25.2 113.3 %copy-start.71 = (f32[704]{0:T(1024)}, f32[704]{0:T(1024)S(1)}, u32[]{:S(2)}) copy-start(f32[704]{0:T(1024)S(1)} %get-tuple-element.255) | copy-start | bytes 8452
  25.2 113.3 %copy-start.73 = (f32[704]{0:T(1024)}, f32[704]{0:T(1024)S(1)}, u32[]{:S(2)}) copy-start(f32[704]{0:T(1024)S(1)} %get-tuple-element.256) | copy-start | bytes 8452
  25.2 113.3 %copy-start.75 = (f32[704]{0:T(1024)}, f32[704]{0:T(1024)S(1)}, u32[]{:S(2)}) copy-start(f32[704]{0:T(1024)S(1)} %get-tuple-element.257) | copy-start | bytes 8452
  25.2 113.3 %copy-start.77 = (f32[704]{0:T(1024)}, f32[704]{0:T(1024)S(1)}, u32[]{:S(2)}) copy-start(f32[704]{0:T(1024)S(1)} %get-tuple-element.258) | copy-start | bytes 8452
  25.9 993.5 %copy-start.49 = (f32[704]{0:T(1024)}, f32[704]{0:T(1024)S(1)}, u32[]{:S(2)}) copy-start(f32[704]{0:T(1024)S(1)} %fusion.94) | copy-start | bytes 8452
  132.6 6.9 copy-start.102
  134.1 4.3 collective-permute-start
  137.2 8.0 copy-start.79
  137.2 8.0 copy-start.81
  137.2 35.1 %copy-start.47 = (f32[4,256]{1,0:T(4,128)}, f32[4,256]{1,0:T(4,128)S(1)}, u32[]{:S(2)}) copy-start(f32[4,256]{1,0:T(4,128)S(1)} %get-tuple-element.377) | copy-start | bytes 12292
  138.4 9.7 copy-start.11
  158.1 14.2 copy-start.4
  179.3 19.8 copy-start.6
  301.5 37.3 %copy-start.67 = (f32[4,1,704]{2,1,0:T(1,128)S(1)}, f32[4,1,704]{2,1,0:T(1,128)}, u32[]{:S(2)}) copy-start(f32[4,1,704]{2,1,0:T(1,128)} %slice.752) | copy-start | bytes 33796
  403.2 6.3 copy-start.70
  545.8 338.1 %all-gather.22.cloned.1.call-start = ((), (), s32[]{:S(2)}) async-start(), calls=%async_computation.13 | async-start | bytes 7077888 | tf_op jit(solution)/shard_map/all_gather | solution.py:101
  546.4 384.9 %all-gather.24.cloned.1.call-start = ((), (), s32[]{:S(2)}) async-start(), calls=%async_computation.14 | async-start | bytes 7077888 | tf_op jit(solution)/shard_map/all_gather | solution.py:102
  547.1 432.8 %all-gather.26.cloned.1.call-start = ((), (), s32[]{:S(2)}) async-start(), calls=%async_computation.15 | async-start | bytes 7077888 | tf_op jit(solution)/shard_map/all_gather | solution.py:103
  547.9 762.5 %all-reduce.75.cloned.1.call-start = ((), (), s32[]{:S(2)}) async-start(), calls=%async_computation.17 | async-start | bytes 16777216 | tf_op jit(solution)/shard_map/psum | solution.py:198
  560.1 750.3 %copy-start.42 = (f32[4,1,512]{2,1,0:T(1,128)}, f32[4,1,512]{2,1,0:T(1,128)S(1)}, u32[]{:S(2)}) copy-start(f32[4,1,512]{2,1,0:T(1,128)S(1)} %convert_element_type.181) | copy-start | bytes 24580
  843.4 467.0 %copy-start.53 = (f32[1024]{0:T(1024)}, f32[1024]{0:T(1024)S(1)}, u32[]{:S(2)}) copy-start(f32[1024]{0:T(1024)S(1)} %fusion.101) | copy-start | bytes 12292
  998.4 10.0 copy-start.112
  998.4 10.0 copy-start.105
  1019.4 915.5 %reduce-scatter.9.cloned.1.call-start = ((), (), s32[]{:S(2)}) async-start(), calls=%async_computation.16 | async-start | bytes 10485760 | tf_op jit(solution)/shard_map/reduce_scatter | solution.py:187
  1103.4 868.7 %reduce-scatter.11.cloned.1.call-start = ((), (), s32[]{:S(2)}) async-start(), calls=%async_computation.18 | async-start | bytes 10485760 | tf_op jit(solution)/shard_map/reduce_scatter | solution.py:277
  1310.4 9.0 copy-start.9
  1310.4 10.2 copy-start.30
  1325.5 11.8 copy-start.15
  1523.2 30.4 %copy-start.66 = (f32[4,1,704]{2,1,0:T(1,128)S(1)}, f32[4,1,704]{2,1,0:T(1,128)}, u32[]{:S(2)}) copy-start(f32[4,1,704]{2,1,0:T(1,128)} %slice.804) | copy-start | bytes 33796
  1531.5 30.1 %copy-start.65 = (f32[4,1,704]{2,1,0:T(1,128)S(1)}, f32[4,1,704]{2,1,0:T(1,128)}, u32[]{:S(2)}) copy-start(f32[4,1,704]{2,1,0:T(1,128)} %slice.829) | copy-start | bytes 33796
  1566.9 10.0 copy-start.69
  1574.4 15.6 copy-start.68
  1615.5 5.7 copy-start.62
  1654.3 5.5 copy-start.61
  1675.2 5.1 copy-start.20
  1675.2 5.4 copy-start.21
  1720.4 24.9 copy-start.39
  1720.4 27.1 %copy-start.5 = (f32[4,256,704]{2,1,0:T(8,128)S(1)}, f32[4,256,704]{2,1,0:T(8,128)}, u32[]{:S(2)}) copy-start(f32[4,256,704]{2,1,0:T(8,128)} %copy-done.4) | copy-start | bytes 8650756
  1720.4 27.1 %copy-start.48 = (f32[4,256]{1,0:T(4,128)S(1)}, f32[4,256]{1,0:T(4,128)}, u32[]{:S(2)}) copy-start(f32[4,256]{1,0:T(4,128)} %copy-done.47) | copy-start | bytes 12292
  1720.4 27.2 %copy-start.50 = (f32[704]{0:T(1024)S(1)}, f32[704]{0:T(1024)}, u32[]{:S(2)}) copy-start(f32[704]{0:T(1024)} %copy-done.49) | copy-start | bytes 8452
  1720.4 27.2 %copy-start.56 = (f32[704]{0:T(1024)S(1)}, f32[704]{0:T(1024)}, u32[]{:S(2)}) copy-start(f32[704]{0:T(1024)} %param.38) | copy-start | bytes 8452
  1720.5 27.2 %copy-start.59 = (f32[704]{0:T(1024)S(1)}, f32[704]{0:T(1024)}, u32[]{:S(2)}) copy-start(f32[704]{0:T(1024)} %param.37) | copy-start | bytes 8452
  1720.5 27.2 %copy-start.60 = (f32[4,1,704]{2,1,0:T(1,128)S(1)}, f32[4,1,704]{2,1,0:T(1,128)}, u32[]{:S(2)}) copy-start(f32[4,1,704]{2,1,0:T(1,128)} %broadcast_in_dim.10) | copy-start | bytes 33796
  1799.4 12.1 copy-start.107
  1799.5 12.1 copy-start.110
  1810.3 5.0 collective-permute-start.1
  1811.7 6.1 copy-start.3
  1826.9 208.0 %all-reduce.77.cloned.1.call-start = ((), (), s32[]{:S(2)}) async-start(), calls=%async_computation.25 | async-start | bytes 2883584 | tf_op jit(solution)/shard_map/psum | solution.py:302
  1831.7 265.9 %reduce-scatter.17.cloned.1.call-start = ((), (), s32[]{:S(2)}) async-start(), calls=%async_computation.21 | async-start | bytes 6488064 | tf_op jit(solution)/shard_map/reduce_scatter | solution.py:287
  1840.8 319.8 %reduce-scatter.13.cloned.1.call-start = ((), (), s32[]{:S(2)}) async-start(), calls=%async_computation.19 | async-start | bytes 6488064 | tf_op jit(solution)/shard_map/reduce_scatter | solution.py:285
  1849.5 374.4 %reduce-scatter.15.cloned.1.call-start = ((), (), s32[]{:S(2)}) async-start(), calls=%async_computation.20 | async-start | bytes 6488064 | tf_op jit(solution)/shard_map/reduce_scatter | solution.py:286
  1858.9 461.3 %reduce-scatter.19.cloned.1.call-start = ((), (), s32[]{:S(2)}) async-start(), calls=%async_computation.22 | async-start | bytes 14155776 | tf_op jit(solution)/shard_map/reduce_scatter | solution.py:288
  1871.5 545.0 %reduce-scatter.21.cloned.1.call-start = ((), (), s32[]{:S(2)}) async-start(), calls=%async_computation.23 | async-start | bytes 14155776 | tf_op jit(solution)/shard_map/reduce_scatter | solution.py:289
  1884.3 628.6 %reduce-scatter.23.cloned.1.call-start = ((), (), s32[]{:S(2)}) async-start(), calls=%async_computation.24 | async-start | bytes 14155776 | tf_op jit(solution)/shard_map/reduce_scatter | solution.py:290
  1896.7 11.8 copy-start.95
  1896.7 11.8 copy-start.96
  1896.7 11.8 copy-start.97
  (69 other events, 214.7 us)
Sparse Core Ops, SparseCore 0:
  9.6 83.4 all-gather.13
  95.0 30.1 all-gather.15
  127.1 31.8 all-gather.17
  160.7 31.6 all-gather.19
  545.9 291.5 all-reduce.72
  839.3 44.5 all-gather.21
  885.7 45.5 all-gather.23
  933.2 46.6 all-gather.25
  1019.5 290.8 all-reduce.74
  1312.6 143.4 reduce-scatter.8
  1827.0 145.0 reduce-scatter.10
  1975.8 59.0 all-reduce.76
  2039.3 58.2 reduce-scatter.16
  2101.5 59.0 reduce-scatter.12
  2164.8 58.9 reduce-scatter.14
  2227.8 92.3 reduce-scatter.18
  2324.1 92.3 reduce-scatter.20
  2420.5 92.3 reduce-scatter.22
where the time goes:
time: 2550 us; the launch traced here: 2520 us
  waiting for transfers between devices  1260 us (49%)
  local copies, waits for them, and re-layouts  706 us (28%)
  other arithmetic  262 us (10%)
  matrix products  194 us (8%)
  blocking collectives  83 us (3%)
    psum x1, waiting for transfers between devices, shards(): rec_total = lax.psum(rec_part, 'tp')  277 us
    slice x57, local copies, waits for them, and re-layouts, shards(): lax.associative_scan(combine, (next_coef, state_direct), reverse=True, ax...  215 us
    psum x1, waiting for transfers between devices, shards(): mid_norm_grad = lax.psum(mid_part, 'tp')  207 us
    slice x52, local copies, waits for them, and re-layouts, shards(): lax.associative_scan(combine, (coeffs, inputs), axis=1)  128 us
    pad x28, local copies, waits for them, and re-layouts, shards(): lax.associative_scan(combine, (coeffs, inputs), axis=1)  110 us
    pad x28, local copies, waits for them, and re-layouts, shards(): lax.associative_scan(combine, (next_coef, state_direct), reverse=True, ax...  108 us
    reduce_scatter x1, waiting for transfers between devices, shards(): lax.psum_scatter(grad_down, ('fsdp', 'ctx'), scatter_dimension=1, tiled=T...  96.4 us
    reduce_scatter x1, waiting for transfers between devices, shards(): lax.psum_scatter(grad_up, ('fsdp', 'ctx'), scatter_dimension=0, tiled=True)  96.3 us
  transfers between devices with their start and end apart: 20, of which 15 were waited for; matrix products, arithmetic and copies ran while one was open for 43% of the time, Pallas kernels for 0%

commit v1 on v0

--- a/solution.py
+++ b/solution.py
@@ -1,10 +1,21 @@
+import functools
 import jax
 import jax.numpy as jnp
 from jax import lax
 from jax.sharding import PartitionSpec as P
+from jax.lax import psum
 
 CONV = 4
 eps_norm = 1e-06
+
+
+def _mix_map(obj, dev_axis, row_axis):
+    for dev_i in (dev_axis, row_axis):
+        obj = psum(obj, axis_name=dev_i)
+    return obj
+
+
+pair_patch_in = functools.partial(_mix_map, dev_axis="ctx", row_axis="fsdp")
 
 
 def from_behind(value, axis, steps):
@@ -299,7 +310,7 @@
         rate_bias_total,
         input_bias_total,
         decay_total,
-    ) = lax.psum(
+    ) = pair_patch_in(
         (
             gain_one_slice,
             gain_two_slice,
@@ -310,8 +321,7 @@
             grad_rate_bias,
             grad_input_bias,
             grad_decay,
-        ),
-        ("fsdp", "ctx"),
+        )
     )
     return (
         block_out,

time: 2550 us -> 2690 us (1.055)
  waiting for transfers between devices: 1260 us -> 1410 us
    reduce_scatter x1, waiting for transfers between devices: 33.6 us -> 144 us  [shards(): lax.psum_scatter(in_from_norm, 'tp', scatter_dimension=1, tiled=True)]
    reduce_scatter x1, waiting for transfers between devices: 0.01 us -> 36.6 us  [shards(): lax.psum_scatter(matmul(hidden, w_down), 'tp', scatter_dimension=1, tiled...]
    psum x1 -> x2, waiting for transfers between devices: 58.8 us -> 47.9 us  [_mix_map(): obj = psum(obj, axis_name=dev_i)]
  transfers between devices with their start and end apart: 20 -> 21, of which waited for: 15 -> 16; matrix products, arithmetic and copies ran while one was open for 43% -> 24% of each run, Pallas kernels for 0% -> 0%
where the time goes in v1:
time: 2690 us; the launch traced here: 2660 us
  waiting for transfers between devices  1410 us (52%)
  local copies, waits for them, and re-layouts  698 us (26%)
  other arithmetic  263 us (10%)
  matrix products  194 us (7%)
  blocking collectives  79.1 us (3%)
    psum x1, waiting for transfers between devices, shards(): rec_total = lax.psum(rec_part, 'tp')  277 us
    psum x1, waiting for transfers between devices, shards(): mid_norm_grad = lax.psum(mid_part, 'tp')  219 us
    slice x57, local copies, waits for them, and re-layouts, shards(): lax.associative_scan(combine, (next_coef, state_direct), reverse=True, ax...  216 us
    reduce_scatter x1, waiting for transfers between devices, shards(): lax.psum_scatter(in_from_norm, 'tp', scatter_dimension=1, tiled=True)  144 us
    slice x52, local copies, waits for them, and re-layouts, shards(): lax.associative_scan(combine, (coeffs, inputs), axis=1)  127 us
    pad x28, local copies, waits for them, and re-layouts, shards(): lax.associative_scan(combine, (coeffs, inputs), axis=1)  109 us
    pad x28, local copies, waits for them, and re-layouts, shards(): lax.associative_scan(combine, (next_coef, state_direct), reverse=True, ax...  108 us
    reduce_scatter x1, waiting for transfers between devices, shards(): lax.psum_scatter(grad_down, ('fsdp', 'ctx'), scatter_dimension=1, tiled=T...  96.5 us
  transfers between devices with their start and end apart: 21, of which 16 were waited for; matrix products, arithmetic and copies ran while one was open for 24% of the time, Pallas kernels for 0%

profile of v1, /device:TPU:0, one launch (start us, length us, event | category | flops | bytes accessed | tf_op | source)
XLA Modules:
  0.0 2662.7 jit_solution(16247939536372966473)
XLA Ops:
  10.7 13.5 all-gather.4
  26.8 66.3 %all-gather.14.cloned.1.call-done = bf16[4,256,2048]{2,1,0:T(8,128)(2,1)} async-done(((bf16[4,256,512]{2,1,0:T(8,128)(2,1)}), bf16[4,256,2048]{2,1,0:T(8,128)(2,1)}) %all-gather.14.cloned.1.call-update) | async-done | bytes 4194320 | tf_op jit(solution)/shard_map/all_gather | solution.py:104
  100.0 25.2 all-gather.16.cloned.1.call-done
  125.2 6.3 convolution_convert_fusion
  172.8 7.1 convert_multiply_fusion.8
  179.9 9.9 slice.580
  189.8 9.6 slice.581
  374.6 9.6 slice.635
  489.5 5.7 pad.229
  515.5 7.2 multiply_add_fusion.2
  526.2 9.7 multiply_convert_fusion.3
  535.8 9.1 fusion.116
  547.1 12.2 all-gather.5
  559.4 277.2 %all-reduce.76.cloned.1.call-done = f32[1024,2048]{1,0:T(8,128)} async-done(((f32[1024,2048]{1,0:T(8,128)}), f32[1024,2048]{1,0:T(8,128)}) %all-reduce.76.cloned.1.call-update) | async-done | bytes 8388624 | tf_op jit(solution)/shard_map/psum | solution.py:190
  836.5 5.7 multiply_reduce_fusion.2
  848.6 34.2 %all-gather.22.cloned.1.call-done = bf16[2048,1536]{1,0:T(8,128)(2,1)} async-done(((bf16[256,1536]{1,0:T(8,128)(2,1)}), bf16[2048,1536]{1,0:T(8,128)(2,1)}) %all-gather.22.cloned.1.call-update) | async-done | bytes 6291472 | tf_op jit(solution)/shard_map/all_gather | solution.py:112
  882.8 12.1 fusion.117
  895.0 35.3 %all-gather.24.cloned.1.call-done = bf16[2048,1536]{1,0:T(8,128)(2,1)} async-done(((bf16[256,1536]{1,0:T(8,128)(2,1)}), bf16[2048,1536]{1,0:T(8,128)(2,1)}) %all-gather.24.cloned.1.call-update) | async-done | bytes 6291472 | tf_op jit(solution)/shard_map/all_gather | solution.py:113
  930.3 11.7 fusion.118
  942.0 36.9 %all-gather.26.cloned.1.call-done = bf16[1536,2048]{1,0:T(8,128)(2,1)} async-done(((bf16[1536,256]{1,0:T(8,128)(2,1)}), bf16[1536,2048]{1,0:T(8,128)(2,1)}) %all-gather.26.cloned.1.call-update) | async-done | bytes 6291472 | tf_op jit(solution)/shard_map/all_gather | solution.py:114
  978.9 18.5 multiply_convert_fusion.1
  997.4 10.0 fusion.120
  1007.4 10.5 convolution_add_fusion.1
  1022.2 9.8 slice.657
  1032.1 9.6 slice.664
  1041.6 9.5 slice.655
  1051.8 12.9 slice.658
  1064.7 12.7 slice.665
  1077.4 12.8 slice.656
  1090.2 218.7 %all-reduce.78.cloned.1.call-done = f32[1024,2048]{1,0:T(8,128)} async-done(((f32[1024,2048]{1,0:T(8,128)}), f32[1024,2048]{1,0:T(8,128)}) %all-reduce.78.cloned.1.call-update) | async-done | bytes 8388624 | tf_op jit(solution)/shard_map/psum | solution.py:209
  1309.0 7.7 multiply_reduce_fusion
  1323.3 11.8 fusion.72
  1338.6 9.6 slice.659
  1348.1 9.5 slice.661
  1357.7 12.8 slice.660
  1370.5 12.8 slice.662
  1482.1 9.5 slice.717
  1632.3 5.8 pad.245
  1638.1 12.9 slice.718
  1657.8 5.7 pad.244
  1702.8 15.6 rev.15
  1718.4 25.0 rev.14
  1743.4 11.9 multiply_reduce_fusion.3
  1774.3 7.6 fusion.60
  1785.9 11.7 fusion.119
  1811.5 10.6 fusion.43
  1840.0 8.2 fusion.62
  1849.6 7.1 fusion.128
  1857.4 8.1 fusion.22
  1865.6 12.6 fusion.122
  1878.3 12.5 fusion.123
  1891.1 12.3 fusion.124
  1906.2 10.3 all-reduce.66
  1916.6 11.3 all-reduce.67
  1927.9 9.1 all-reduce.69
  1937.0 36.6 %reduce-scatter.9.cloned.1.call-done = f32[1024,512]{1,0:T(8,128)} async-done(((f32[1024,2048]{1,0:T(8,128)}), f32[1024,512]{1,0:T(8,128)}) %reduce-scatter.9.cloned.1.call-update) | async-done | bytes 2097168 | tf_op jit(solution)/shard_map/reduce_scatter | solution.py:198
  1977.1 143.9 %reduce-scatter.11.cloned.1.call-done = f32[1024,512]{1,0:T(8,128)} async-done(((f32[1024,2048]{1,0:T(8,128)}), f32[1024,512]{1,0:T(8,128)}) %reduce-scatter.11.cloned.1.call-update) | async-done | bytes 2097168 | tf_op jit(solution)/shard_map/reduce_scatter | solution.py:288
  2125.0 47.9 %all-reduce.82.cloned.1.call-done = (f32[4,176,176]{2,1,0:T(8,128)}, f32[4,176,176]{2,1,0:T(8,128)}) async-done(((f32[4,176,176]{2,1,0:T(8,128)}, f32[4,176,176]{2,1,0:T(8,128)}), (f32[4,176,176]{2,1,0:T(8,128)}, f32[4,176,176]{2,1,0:T(8,128)})) %all-reduce.82.cloned.1.call-update) | async-done | bytes 991248 | tf_op jit(solution)/shard_map/psum | solution.py:14
  2172.9 63.4 %reduce-scatter.17.cloned.1.call-done = f32[704,256]{1,0:T(8,128)} async-done(((f32[704,2048]{1,0:T(8,128)}), f32[704,256]{1,0:T(8,128)}) %reduce-scatter.17.cloned.1.call-update) | async-done | bytes 720912 | tf_op jit(solution)/shard_map/reduce_scatter | solution.py:298
  2236.2 62.9 %reduce-scatter.13.cloned.1.call-done = f32[256,704]{0,1:T(8,128)} async-done(((f32[2048,704]{0,1:T(8,128)}), f32[256,704]{0,1:T(8,128)}) %reduce-scatter.13.cloned.1.call-update) | async-done | bytes 720912 | tf_op jit(solution)/shard_map/reduce_scatter | solution.py:296
  2299.1 63.3 %reduce-scatter.15.cloned.1.call-done = f32[256,704]{0,1:T(8,128)} async-done(((f32[2048,704]{0,1:T(8,128)}), f32[256,704]{0,1:T(8,128)}) %reduce-scatter.15.cloned.1.call-update) | async-done | bytes 720912 | tf_op jit(solution)/shard_map/reduce_scatter | solution.py:297
  2362.5 96.3 %reduce-scatter.19.cloned.1.call-done = f32[256,1536]{1,0:T(8,128)} async-done(((f32[2048,1536]{1,0:T(8,128)}), f32[256,1536]{1,0:T(8,128)}) %reduce-scatter.19.cloned.1.call-update) | async-done | bytes 1572880 | tf_op jit(solution)/shard_map/reduce_scatter | solution.py:299
  2458.8 96.4 %reduce-scatter.21.cloned.1.call-done = f32[256,1536]{1,0:T(8,128)} async-done(((f32[2048,1536]{1,0:T(8,128)}), f32[256,1536]{1,0:T(8,128)}) %reduce-scatter.21.cloned.1.call-update) | async-done | bytes 1572880 | tf_op jit(solution)/shard_map/reduce_scatter | solution.py:300
  2555.2 96.5 %reduce-scatter.23.cloned.1.call-done = f32[1536,256]{1,0:T(8,128)} async-done(((f32[1536,2048]{1,0:T(8,128)}), f32[1536,256]{1,0:T(8,128)}) %reduce-scatter.23.cloned.1.call-update) | async-done | bytes 1572880 | tf_op jit(solution)/shard_map/reduce_scatter | solution.py:301
  (595 shorter events, 741.8 us)
Async XLA Ops:
  7.2 141.4 %copy-start = (bf16[4,176,176]{2,1,0:T(8,128)(2,1)S(1)}, bf16[4,176,176]{2,1,0:T(8,128)(2,1)}, u32[]{:S(2)}) copy-start(bf16[4,176,176]{2,1,0:T(8,128)(2,1)} %param.35) | copy-start | bytes 743428
  7.2 85.9 %all-gather.14.cloned.1.call-start = ((), (), s32[]{:S(2)}) async-start(), calls=%async_computation.8 | async-start | bytes 5242880 | tf_op jit(solution)/shard_map/all_gather | solution.py:104
  7.9 117.3 %all-gather.16.cloned.1.call-start = ((), (), s32[]{:S(2)}) async-start(), calls=%async_computation.9 | async-start | bytes 3244032 | tf_op jit(solution)/shard_map/all_gather | solution.py:110
  8.7 517.5 %all-gather.18.cloned.1.call-start = ((), (), s32[]{:S(2)}) async-start(), calls=%async_computation.10 | async-start | bytes 3244032 | tf_op jit(solution)/shard_map/all_gather | solution.py:109
  9.4 526.4 %all-gather.20.cloned.1.call-start = ((), (), s32[]{:S(2)}) async-start(), calls=%async_computation.11 | async-start | bytes 3244032 | tf_op jit(solution)/shard_map/all_gather | solution.py:111
  10.0 826.5 %all-reduce.76.cloned.1.call-start = ((), (), s32[]{:S(2)}) async-start(), calls=%async_computation.12 | async-start | bytes 16777216 | tf_op jit(solution)/shard_map/psum | solution.py:190
  24.3 75.7 %copy-start.45 = (f32[4,1,512]{2,1,0:T(1,128)}, f32[4,1,512]{2,1,0:T(1,128)S(1)}, u32[]{:S(2)}) copy-start(f32[4,1,512]{2,1,0:T(1,128)S(1)} %convert_element_type.180) | copy-start | bytes 24580
  25.2 113.6 %copy-start.67 = (f32[704]{0:T(1024)}, f32[704]{0:T(1024)S(1)}, u32[]{:S(2)}) copy-start(f32[704]{0:T(1024)S(1)} %get-tuple-element.255) | copy-start | bytes 8452
  25.2 113.6 %copy-start.69 = (f32[704]{0:T(1024)}, f32[704]{0:T(1024)S(1)}, u32[]{:S(2)}) copy-start(f32[704]{0:T(1024)S(1)} %get-tuple-element.256) | copy-start | bytes 8452
  25.2 113.6 %copy-start.71 = (f32[704]{0:T(1024)}, f32[704]{0:T(1024)S(1)}, u32[]{:S(2)}) copy-start(f32[704]{0:T(1024)S(1)} %get-tuple-element.257) | copy-start | bytes 8452
  25.2 113.6 %copy-start.73 = (f32[704]{0:T(1024)}, f32[704]{0:T(1024)S(1)}, u32[]{:S(2)}) copy-start(f32[704]{0:T(1024)S(1)} %get-tuple-element.258) | copy-start | bytes 8452
  25.9 992.1 %copy-start.43 = (f32[704]{0:T(1024)}, f32[704]{0:T(1024)S(1)}, u32[]{:S(2)}) copy-start(f32[704]{0:T(1024)S(1)} %fusion.94) | copy-start | bytes 8452
  132.6 7.4 copy-start.98
  134.2 4.6 collective-permute-start
  137.5 8.1 copy-start.75
  137.5 8.1 copy-start.77
  137.5 35.3 %copy-start.41 = (f32[4,256]{1,0:T(4,128)}, f32[4,256]{1,0:T(4,128)S(1)}, u32[]{:S(2)}) copy-start(f32[4,256]{1,0:T(4,128)S(1)} %get-tuple-element.386) | copy-start | bytes 12292
  138.8 9.8 copy-start.11
  158.7 14.1 copy-start.4
  179.9 19.5 copy-start.6
  301.7 37.1 %copy-start.61 = (f32[4,1,704]{2,1,0:T(1,128)S(1)}, f32[4,1,704]{2,1,0:T(1,128)}, u32[]{:S(2)}) copy-start(f32[4,1,704]{2,1,0:T(1,128)} %slice.752) | copy-start | bytes 33796
  403.0 6.3 copy-start.66
  544.9 337.9 %all-gather.22.cloned.1.call-start = ((), (), s32[]{:S(2)}) async-start(), calls=%async_computation.13 | async-start | bytes 7077888 | tf_op jit(solution)/shard_map/all_gather | solution.py:112
  545.5 384.8 %all-gather.24.cloned.1.call-start = ((), (), s32[]{:S(2)}) async-start(), calls=%async_computation.14 | async-start | bytes 7077888 | tf_op jit(solution)/shard_map/all_gather | solution.py:113
  546.3 432.6 %all-gather.26.cloned.1.call-start = ((), (), s32[]{:S(2)}) async-start(), calls=%async_computation.15 | async-start | bytes 7077888 | tf_op jit(solution)/shard_map/all_gather | solution.py:114
  547.0 761.9 %all-reduce.78.cloned.1.call-start = ((), (), s32[]{:S(2)}) async-start(), calls=%async_computation.17 | async-start | bytes 16777216 | tf_op jit(solution)/shard_map/psum | solution.py:209
  559.3 749.6 %copy-start.40 = (f32[4,1,512]{2,1,0:T(1,128)}, f32[4,1,512]{2,1,0:T(1,128)S(1)}, u32[]{:S(2)}) copy-start(f32[4,1,512]{2,1,0:T(1,128)S(1)} %convert_element_type.181) | copy-start | bytes 24580
  842.3 466.7 %copy-start.47 = (f32[1024]{0:T(1024)}, f32[1024]{0:T(1024)S(1)}, u32[]{:S(2)}) copy-start(f32[1024]{0:T(1024)S(1)} %fusion.101) | copy-start | bytes 12292
  997.4 10.0 copy-start.108
  997.4 10.0 copy-start.101
  1018.0 820.8 %all-reduce.80.cloned.1.call-start = ((), (), s32[]{:S(2)}) async-start(), calls=%async_computation.25 | async-start | bytes 2883584 | tf_op jit(solution)/shard_map/psum | solution.py:14
  1308.9 8.4 copy-start.9
  1309.0 9.4 copy-start.30
  1323.3 11.8 copy-start.15
  1472.1 21.0 copy-start.62
  1472.1 21.0 copy-start.63
  1519.4 30.4 %copy-start.60 = (f32[4,1,704]{2,1,0:T(1,128)S(1)}, f32[4,1,704]{2,1,0:T(1,128)}, u32[]{:S(2)}) copy-start(f32[4,1,704]{2,1,0:T(1,128)} %slice.804) | copy-start | bytes 33796
  1527.6 30.1 %copy-start.59 = (f32[4,1,704]{2,1,0:T(1,128)S(1)}, f32[4,1,704]{2,1,0:T(1,128)}, u32[]{:S(2)}) copy-start(f32[4,1,704]{2,1,0:T(1,128)} %slice.829) | copy-start | bytes 33796
  1563.1 10.0 copy-start.65
  1570.6 15.6 copy-start.64
  1678.3 22.2 copy-start.37
  1678.3 24.5 copy-start.21
  1718.4 25.0 copy-start.5
  1718.4 25.0 copy-start.42
  1718.4 25.0 copy-start.44
  1718.4 25.0 copy-start.50
  1718.4 25.0 copy-start.53
  1718.4 25.0 copy-start.54
  1774.3 8.7 copy-start.8
  1785.8 187.7 %reduce-scatter.9.cloned.1.call-start = ((), (), s32[]{:S(2)}) async-start(), calls=%async_computation.16 | async-start | bytes 10485760 | tf_op jit(solution)/shard_map/reduce_scatter | solution.py:198
  1797.6 323.4 %reduce-scatter.11.cloned.1.call-start = ((), (), s32[]{:S(2)}) async-start(), calls=%async_computation.18 | async-start | bytes 10485760 | tf_op jit(solution)/shard_map/reduce_scatter | solution.py:288
  1811.5 11.9 copy-start.103
  1811.5 11.9 copy-start.106
  1822.1 5.0 collective-permute-start.1
  1838.7 334.2 %all-reduce.82.cloned.1.call-start = ((), (), s32[]{:S(2)}) async-start(), calls=%async_computation.26 | async-start | bytes 2883584 | tf_op jit(solution)/shard_map/psum | solution.py:14
  1839.4 396.8 %reduce-scatter.17.cloned.1.call-start = ((), (), s32[]{:S(2)}) async-start(), calls=%async_computation.21 | async-start | bytes 6488064 | tf_op jit(solution)/shard_map/reduce_scatter | solution.py:298
  1848.3 450.9 %reduce-scatter.13.cloned.1.call-start = ((), (), s32[]{:S(2)}) async-start(), calls=%async_computation.19 | async-start | bytes 6488064 | tf_op jit(solution)/shard_map/reduce_scatter | solution.py:296
  1856.7 505.8 %reduce-scatter.15.cloned.1.call-start = ((), (), s32[]{:S(2)}) async-start(), calls=%async_computation.20 | async-start | bytes 6488064 | tf_op jit(solution)/shard_map/reduce_scatter | solution.py:297
  1865.5 593.3 %reduce-scatter.19.cloned.1.call-start = ((), (), s32[]{:S(2)}) async-start(), calls=%async_computation.22 | async-start | bytes 14155776 | tf_op jit(solution)/shard_map/reduce_scatter | solution.py:299
  1878.2 676.9 %reduce-scatter.21.cloned.1.call-start = ((), (), s32[]{:S(2)}) async-start(), calls=%async_computation.23 | async-start | bytes 14155776 | tf_op jit(solution)/shard_map/reduce_scatter | solution.py:300
  1890.8 760.8 %reduce-scatter.23.cloned.1.call-start = ((), (), s32[]{:S(2)}) async-start(), calls=%async_computation.24 | async-start | bytes 14155776 | tf_op jit(solution)/shard_map/reduce_scatter | solution.py:301
  1903.4 13.2 copy-start.91
  1903.4 13.2 copy-start.92
  1903.5 13.2 copy-start.93
  (66 other events, 227.3 us)
Sparse Core Ops, SparseCore 0:
  9.6 83.4 all-gather.13
  95.0 30.1 all-gather.15
  127.1 31.8 all-gather.17
  160.7 31.6 all-gather.19
  545.1 291.4 all-reduce.75
  838.3 44.5 all-gather.21
  884.7 45.5 all-gather.23
  932.1 46.6 all-gather.25
  1018.1 290.8 all-reduce.77
  1785.9 39.9 all-reduce.79
  1828.3 145.1 reduce-scatter.8
  1975.7 145.2 reduce-scatter.10
  2123.3 49.5 all-reduce.81
  2177.2 59.0 reduce-scatter.16
  2240.1 58.9 reduce-scatter.12
  2303.4 59.0 reduce-scatter.14
  2366.4 92.3 reduce-scatter.18
  2462.7 92.3 reduce-scatter.20
  2559.2 92.3 reduce-scatter.22
